TPU v7x, 32 devices: a whole 2x2x4 slice. The times are simulated.
32 devices in a mesh: groups: 2 (over x), ctx: 16 (over z, y, core).
Axes of the slice: x: 2, y: 2, z: 4, core: 2. Of those that a mesh axis runs over, the one named last changes fastest.
Arguments:
- tokens: bfloat16 [16384, 1024], P(('groups', 'ctx')), parts along dimension 0
- w_qkv: bfloat16 [1024, 3072], P('ctx'), may hold values from -0.1875 to 0.1875
- w_out: bfloat16 [1024, 1024], P('ctx'), may hold values from -0.1875 to 0.1875
- var_bias: float32 [2, 16], replicated, may hold values from -2 to 2
- seg_id: int32 [16384], P(('groups', 'ctx')), parts along dimension 0, may hold values from 0 to 3, as said below
- var_id: int32 [16384], P(('groups', 'ctx')), parts along dimension 0, may hold values from 0 to 511
- time_id: int32 [16384], P(('groups', 'ctx')), parts along dimension 0, may hold values from 0 to 67
Outputs:
- mixed: bfloat16 [16384, 1024], P(('groups', 'ctx')), parts along dimension 0
There are 2 independent parts, one for each index of `groups`. A program takes and returns all parts, laid end to end along the dimension named above; an argument that names none is the same for every part. Nothing has to cross between parts.
Inputs may be any that keep to these rules, and one draw needn't show every extreme that they name: seg_id starts at 0, never falls, and rises by at most one from a token to the next.
All inputs are finite; a program needn't handle non-finite values.
Results may differ from a plain program's by a relative error of at most 0.004.
The roundings to bfloat16 on the way count: a program that leaves them out, or rounds other values in their place, can miss the bound.
Values may be sent and summed in bfloat16 or wider, within the bound.
No kernel may reach another device: no remote copies, remote signals or barrier semaphores. Data moves between devices by JAX's collectives and lax.ppermute only.
A program may use at most 256 MiB of HBM per device.

v0:
```python
import math
import jax
import jax.numpy as jnp
from jax import lax
from jax.sharding import PartitionSpec as P


def as_sent(value):
    return jax.tree.map(lambda a: a.astype(jnp.bfloat16) if a.dtype == jnp.float32 else a, value)


def passed_along(value, axis, by):
    devices = lax.axis_size(axis)
    return lax.ppermute(value, axis, [(i, (i + by) % devices) for i in range(devices)])


def gather_near(payload):

    def relay(item, step):
        return passed_along((item[0], as_sent(item[1])), "ctx", step)

    before_one = relay(payload, 1)
    before_two = relay(before_one, 1)
    after_one = relay(payload, -1)
    after_two = relay(after_one, -1)
    return (before_two, before_one, after_one, after_two)


def local(tokens, w_qkv, w_out, var_bias, seg_id, var_id, time_id):
    rows = tokens.shape[0]
    width = tokens.shape[1]
    heads = var_bias.shape[1]
    hsize = width // heads
    idents = jnp.stack([seg_id, var_id, time_id], 0)
    center = lax.axis_index("ctx")
    count = lax.axis_size("ctx")
    columns = tokens
    qkv = jnp.dot(
        columns,
        lax.all_gather(w_qkv, "ctx", axis=0, tiled=True),
        preferred_element_type=jnp.float32,
    )
    qkv = qkv.astype(jnp.bfloat16)
    query = qkv[:, :width]
    keyval = qkv[:, width:]
    near = gather_near((keyval, idents))
    kv_list = [near[0][0], near[1][0], keyval, near[2][0], near[3][0]]
    id_list = [near[0][1], near[1][1], idents, near[2][1], near[3][1]]
    win_kv = jnp.concatenate(kv_list, 0)
    win_ids = jnp.concatenate(id_list, 1)
    span = 5 * rows
    q_pos = center * rows + jnp.arange(rows, dtype=jnp.int32)
    k_pos = (center - 2) * rows + jnp.arange(span, dtype=jnp.int32)
    inside = (k_pos >= 0) & (k_pos < count * rows)
    allowed = (seg_id[:, None] == win_ids[0][None, :]) & (win_ids[2][None, :] <= time_id[:, None])
    allowed = allowed & (jnp.abs(q_pos[:, None] - k_pos[None, :]) <= 2 * rows - 1) & inside[None, :]
    same = var_id[:, None] == win_ids[1][None, :]
    query_heads = query.reshape(rows, heads, hsize)
    key_heads = win_kv[:, :width].reshape(span, heads, hsize)
    value_heads = win_kv[:, width:].reshape(span, heads, hsize)
    scale = 1.0 / math.sqrt(hsize)
    group = math.gcd(4, heads)
    results = []
    for first in range(0, heads, group):
        q_grp = query_heads[:, first : first + group]
        k_grp = key_heads[:, first : first + group]
        v_grp = value_heads[:, first : first + group]
        bias = jnp.where(
            same[None, :, :],
            var_bias[0, first : first + group][:, None, None],
            var_bias[1, first : first + group][:, None, None],
        )
        score = (
            jnp.einsum("qhe,khe->hqk", q_grp, k_grp, preferred_element_type=jnp.float32) * scale
            + bias
        )
        score = jnp.where(allowed[None, :, :], score, -1e30)
        peak = jnp.max(score, axis=-1, keepdims=True)
        weight = jnp.where(allowed[None, :, :], jnp.exp(score - peak), 0.0)
        total = jnp.sum(weight, axis=-1)
        weight_bf = weight.astype(jnp.bfloat16)
        summed = jnp.einsum("hqk,khe->qhe", weight_bf, v_grp, preferred_element_type=jnp.float32)
        results.append(summed / jnp.transpose(total)[:, :, None])
    attended = jnp.concatenate(results, 1).reshape(rows, width).astype(jnp.bfloat16)
    columns = attended
    mixed = jnp.dot(
        columns,
        lax.all_gather(w_out, "ctx", axis=0, tiled=True),
        preferred_element_type=jnp.float32,
    )
    return mixed.astype(jnp.bfloat16)


def solution(mesh):
    in_specs = (
        P(("groups", "ctx"), None),
        P("ctx", None),
        P("ctx", None),
        P(),
        P(("groups", "ctx")),
        P(("groups", "ctx")),
        P(("groups", "ctx")),
    )
    out_specs = P(("groups", "ctx"), None)
    return jax.shard_map(local, mesh=mesh, in_specs=in_specs, out_specs=out_specs, check_vma=False)
```

profile of v0, /device:TPU:1, one launch (start us, length us, event | category | flops | bytes accessed | tf_op | source)
XLA Modules:
  0.0 518.6 jit_solution(13979249160202723776)
XLA Ops:
  6.5 0.7 all-gather.3.cloned.1.call-update
  7.3 0.0 all-gather.5.cloned.1.call-start
  7.3 66.7 %all-gather.3.cloned.1.call-done = bf16[1024,3072]{1,0:T(8,128)(2,1)} async-done(((bf16[64,3072]{1,0:T(8,128)(2,1)}), bf16[1024,3072]{1,0:T(8,128)(2,1)}) %all-gather.3.cloned.1.call-update) | async-done | bytes 6291472 | tf_op jit(solution)/shard_map/all_gather | solution.py:40
  74.0 6.4 %convolution_convert_fusion = bf16[512,3072]{1,0:T(8,128)(2,1)S(1)} fusion(bf16[512,1024]{1,0:T(8,128)(2,1)S(1)} %copy-done, bf16[1024,3072]{1,0:T(8,128)(2,1)} %all-gather.3.cloned.1.call-done), kind=kOutput, calls=%fused_computation.51 | convolution fusion | flops 3222798336 | bytes 10485760 | tf_op jit(solution)/shard_map/dot_general | solution.py:38
  80.4 1.7 copy-done.2
  82.2 1.5 slice.117
  83.7 0.4 collective-permute-start
  84.1 0.1 collective-permute-start.2
  84.2 1.7 collective-permute-start.4
  85.9 2.6 collective-permute-start.6
  88.5 0.0 all-gather.5.cloned.1.call-update
  88.6 0.6 slice_bitcast_fusion.7
  89.2 47.8 %collective-permute-done.4 = s32[3,512]{1,0:T(4,128)S(1)} collective-permute-done((s32[3,512]{1,0:T(4,128)S(1)}, s32[3,512]{1,0:T(4,128)S(1)}, u32[]{:S(2)}, u32[]{:S(2)}) %collective-permute-start.4) | collective-permute-done | bytes 6176 | tf_op jit(solution)/shard_map/ppermute | solution.py:14
  137.0 2.5 collective-permute-start.5
  139.4 0.5 collective-permute-done.6
  139.9 1.7 collective-permute-start.1
  141.7 2.5 collective-permute-done.7
  144.2 0.1 slice_reduce_fusion.2
  144.3 5.6 %fusion.41 = pred[512,2560]{1,0:T(8,128)(4,1)} fusion(s32[2560]{0:T(1024)S(1)} %iota_add_fusion, s32[512]{0:T(512)S(1)} %iota_add_fusion.1, s32[2560]{0:T(1024)S(1)} %get-tuple-element.7, s32[2560]{0:T(1024)S(1)} %get-tuple-element.5, s32[512]{0:T(512)S(1)} %copy-done.6, s32[512]{0:T(512)S(1)} %copy-done.7, pred[2560]{0:T(1024)(128)(4,1)S(1)} %compare_and_fusion), kind=kLoop, calls=%fused_computation.50 | loop fusion | flops 10485760 | bytes 1350144 | tf_op jit(solution)/shard_map/and | solution.py:56
  149.9 0.5 collective-permute-start.3
  150.3 2.0 broadcast_compare_fusion
  152.3 1.3 slice.121
  153.6 1.3 copy.21
  154.9 32.5 %collective-permute-done.1 = bf16[512,2048]{1,0:T(8,128)(2,1)} collective-permute-done((bf16[512,2048]{1,0:T(8,128)(2,1)}, bf16[512,2048]{1,0:T(8,128)(2,1)}, u32[]{:S(2)}, u32[]{:S(2)}) %collective-permute-start.1) | collective-permute-done | bytes 2097184 | tf_op jit(solution)/shard_map/ppermute | solution.py:14
  187.4 3.2 constant_dynamic-update-slice_fusion.4
  190.6 3.1 constant_dynamic-update-slice_fusion.3
  193.7 3.2 constant_dynamic-update-slice_fusion.2
  196.9 1.5 constant_dynamic-update-slice_fusion.1
  198.4 3.2 constant_dynamic-update-slice_fusion
  201.6 9.2 %fusion.118 = (bf16[2560,1024]{1,0:T(8,128)(2,1)}, bf16[2560,1024]{1,0:T(8,128)(2,1)}) fusion(bf16[2560,2048]{1,0:T(8,128)(2,1)} %constant_dynamic-update-slice_fusion), kind=kLoop, calls=%fused_computation.124 | loop fusion | bytes 20971520 | tf_op jit(solution)/shard_map/slice | solution.py:59
  210.9 8.0 %copy.22 = bf16[2560,1024]{0,1:T(8,128)(2,1)} copy(bf16[2560,1024]{1,0:T(8,128)(2,1)} %get-tuple-element.8) | data formatting | bytes 10485760 | tf_op jit(solution)/shard_map/slice | solution.py:59
  218.9 10.1 %fusion.42 = f32[4,512,2560]{2,1,0:T(8,128)} fusion(bf16[512,16,64]{0,2,1:T(8,128)(2,1)S(1)} %bitcast.72, bf16[2560,16,64]{0,2,1:T(8,128)(2,1)} %bitcast.67), kind=kOutput, calls=%fused_computation.54 | convolution fusion | flops 671088640 | bytes 23330816 | tf_op jit(solution)/shard_map/qhe,khe->hqk/dot_general | solution.py:74
  229.0 8.8 %fusion.44 = f32[4,512,2560]{2,1,0:T(8,128)} fusion(bf16[512,16,64]{0,2,1:T(8,128)(2,1)S(1)} %bitcast.73, bf16[2560,16,64]{0,2,1:T(8,128)(2,1)S(1)} %bitcast.68), kind=kOutput, calls=%fused_computation.56 | convolution fusion | flops 671088640 | bytes 23330816 | tf_op jit(solution)/shard_map/qhe,khe->hqk/dot_general | solution.py:74
  237.8 8.6 %fusion.46 = f32[4,512,2560]{2,1,0:T(8,128)} fusion(bf16[512,16,64]{0,2,1:T(8,128)(2,1)S(1)} %bitcast.74, bf16[2560,16,64]{0,2,1:T(8,128)(2,1)S(1)} %bitcast.69), kind=kOutput, calls=%fused_computation.58 | convolution fusion | flops 671088640 | bytes 23330816 | tf_op jit(solution)/shard_map/qhe,khe->hqk/dot_general | solution.py:74
  246.4 8.7 %fusion.48 = f32[4,512,2560]{2,1,0:T(8,128)} fusion(bf16[512,16,64]{0,2,1:T(8,128)(2,1)S(1)} %bitcast.75, bf16[2560,16,64]{0,2,1:T(8,128)(2,1)S(1)} %bitcast.70), kind=kOutput, calls=%fused_computation.60 | convolution fusion | flops 671088640 | bytes 23330816 | tf_op jit(solution)/shard_map/qhe,khe->hqk/dot_general | solution.py:74
  255.1 7.9 %copy.20 = bf16[2560,1024]{0,1:T(8,128)(2,1)} copy(bf16[2560,1024]{1,0:T(8,128)(2,1)} %get-tuple-element.9) | data formatting | bytes 10485760 | tf_op jit(solution)/shard_map/slice | solution.py:60
  263.0 31.4 %fusion.119 = f32[4,512]{1,0:T(4,128)S(1)} fusion(f32[4,512,2560]{2,1,0:T(8,128)} %fusion.42, f32[4]{0:T(128)S(1)} %get-tuple-element.16, f32[4]{0:T(128)S(1)} %get-tuple-element.17, pred[512,2560]{1,0:T(8,128)(4,1)} %broadcast_compare_fusion, pred[512,2560]{1,0:T(8,128)(4,1)S(1)} %copy-done.4), kind=kOutput, calls=%fused_computation.125 | output fusion | flops 36702720 | bytes 23601184 | tf_op jit(solution)/shard_map/sub | solution.py:79
  294.4 29.6 %fusion.65 = bf16[512,4,64]{0,2,1:T(8,128)(2,1)S(1)} fusion(bf16[2560,16,64]{0,2,1:T(8,128)(2,1)} %bitcast.63, f32[4,512,2560]{2,1,0:T(8,128)} %fusion.42, f32[4]{0:T(128)S(1)} %get-tuple-element.16, f32[4]{0:T(128)S(1)} %get-tuple-element.17, pred[512,2560]{1,0:T(8,128)(4,1)} %broadcast_compare_fusion, pred[512,2560]{1,0:T(8,128)(4,1)S(1)} %copy-done.4, ...), kind=kOutput, calls=%fused_computation.68 | convolution fusion | flops 708055552 | bytes 29106208 | tf_op jit(solution)/shard_map/hqk,khe->qhe/dot_general | solution.py:82
  324.0 31.1 %fusion.120 = f32[4,512]{1,0:T(4,128)S(1)} fusion(f32[4,512,2560]{2,1,0:T(8,128)} %fusion.44, f32[4]{0:T(128)S(1)} %get-tuple-element.11, f32[4]{0:T(128)S(1)} %get-tuple-element.12, pred[512,2560]{1,0:T(8,128)(4,1)} %broadcast_compare_fusion, pred[512,2560]{1,0:T(8,128)(4,1)S(1)} %copy-done.4), kind=kOutput, calls=%fused_computation.126 | output fusion | flops 36702720 | bytes 23601184 | tf_op jit(solution)/shard_map/sub | solution.py:79
  355.1 29.7 %fusion.71 = bf16[512,4,64]{0,2,1:T(8,128)(2,1)S(1)} fusion(bf16[2560,16,64]{0,2,1:T(8,128)(2,1)} %bitcast.64, f32[4,512,2560]{2,1,0:T(8,128)} %fusion.44, f32[4]{0:T(128)S(1)} %get-tuple-element.11, f32[4]{0:T(128)S(1)} %get-tuple-element.12, pred[512,2560]{1,0:T(8,128)(4,1)} %broadcast_compare_fusion, pred[512,2560]{1,0:T(8,128)(4,1)S(1)} %copy-done.4, ...), kind=kOutput, calls=%fused_computation.70 | convolution fusion | flops 708055552 | bytes 29106208 | tf_op jit(solution)/shard_map/hqk,khe->qhe/dot_general | solution.py:82
  384.8 31.7 %fusion.121 = f32[4,512]{1,0:T(4,128)S(1)} fusion(f32[4,512,2560]{2,1,0:T(8,128)} %fusion.46, f32[4]{0:T(128)S(1)} %get-tuple-element.13, f32[4]{0:T(128)S(1)} %get-tuple-element.14, pred[512,2560]{1,0:T(8,128)(4,1)} %broadcast_compare_fusion, pred[512,2560]{1,0:T(8,128)(4,1)S(1)} %copy-done.4), kind=kOutput, calls=%fused_computation.127 | output fusion | flops 36702720 | bytes 23601184 | tf_op jit(solution)/shard_map/sub | solution.py:79
  416.5 29.5 %fusion.77 = bf16[512,4,64]{0,2,1:T(8,128)(2,1)S(1)} fusion(bf16[2560,16,64]{0,2,1:T(8,128)(2,1)} %bitcast.65, f32[4,512,2560]{2,1,0:T(8,128)} %fusion.46, f32[4]{0:T(128)S(1)} %get-tuple-element.13, f32[4]{0:T(128)S(1)} %get-tuple-element.14, pred[512,2560]{1,0:T(8,128)(4,1)} %broadcast_compare_fusion, pred[512,2560]{1,0:T(8,128)(4,1)S(1)} %copy-done.4, ...), kind=kOutput, calls=%fused_computation.72 | convolution fusion | flops 708055552 | bytes 29106208 | tf_op jit(solution)/shard_map/hqk,khe->qhe/dot_general | solution.py:82
  446.0 31.6 %fusion.122 = f32[4,512]{1,0:T(4,128)S(1)} fusion(f32[4,512,2560]{2,1,0:T(8,128)} %fusion.48, f32[4]{0:T(128)S(1)} %copy-done.11, f32[4]{0:T(128)S(1)} %copy-done.10, pred[512,2560]{1,0:T(8,128)(4,1)} %broadcast_compare_fusion, pred[512,2560]{1,0:T(8,128)(4,1)S(1)} %copy-done.4), kind=kOutput, calls=%fused_computation.128 | output fusion | flops 36702720 | bytes 23601184 | tf_op jit(solution)/shard_map/sub | solution.py:79
  477.6 0.0 copy-start.1
  477.6 29.9 %fusion.83 = bf16[512,4,64]{0,2,1:T(8,128)(2,1)S(1)} fusion(bf16[2560,16,64]{0,2,1:T(8,128)(2,1)} %bitcast.66, f32[4,512,2560]{2,1,0:T(8,128)} %fusion.48, f32[4]{0:T(128)S(1)} %copy-done.11, f32[4]{0:T(128)S(1)} %copy-done.10, pred[512,2560]{1,0:T(8,128)(4,1)} %broadcast_compare_fusion, pred[512,2560]{1,0:T(8,128)(4,1)S(1)} %copy-done.4, ...), kind=kOutput, calls=%fused_computation.74 | convolution fusion | flops 708055552 | bytes 29106208 | tf_op jit(solution)/shard_map/hqk,khe->qhe/dot_general | solution.py:82
  507.5 0.1 pad_maximum_fusion
  507.7 0.0 all-gather.5.cloned.1.call-done
  507.7 3.8 convolution_convert_fusion.1
  (37 shorter events, 0.1 us)
Async XLA Ops:
  6.5 67.5 %copy-start = (bf16[512,1024]{1,0:T(8,128)(2,1)S(1)}, bf16[512,1024]{1,0:T(8,128)(2,1)}, u32[]{:S(2)}) copy-start(bf16[512,1024]{1,0:T(8,128)(2,1)} %param.7) | copy-start | bytes 3145732
  6.5 67.5 %all-gather.3.cloned.1.call-start = ((), (), s32[]{:S(2)}) async-start(), calls=%async_computation | async-start | bytes 6684672 | tf_op jit(solution)/shard_map/all_gather | solution.py:40
  7.3 76.9 %copy-start.6 = (s32[512]{0:T(512)S(1)}, s32[512]{0:T(512)}, u32[]{:S(2)}) copy-start(s32[512]{0:T(512)} %param.13) | copy-start | bytes 6148
  7.3 76.9 %copy-start.7 = (s32[512]{0:T(512)S(1)}, s32[512]{0:T(512)}, u32[]{:S(2)}) copy-start(s32[512]{0:T(512)} %param.11) | copy-start | bytes 6148
  7.3 76.9 %copy-start.8 = (s32[512]{0:T(512)S(1)}, s32[512]{0:T(512)}, u32[]{:S(2)}) copy-start(s32[512]{0:T(512)} %param.12) | copy-start | bytes 6148
  7.3 81.3 %copy-start.9 = (f32[2,16]{1,0:T(2,128)S(1)}, f32[2,16]{1,0:T(2,128)}, u32[]{:S(2)}) copy-start(f32[2,16]{1,0:T(2,128)} %param.10) | copy-start | bytes 388
  7.3 500.4 %all-gather.5.cloned.1.call-start = ((), (), s32[]{:S(2)}) async-start(), calls=%async_computation.1 | async-start | bytes 2228224 | tf_op jit(solution)/shard_map/all_gather | solution.py:88
  80.4 1.8 copy-start.2
  83.7 56.2 %collective-permute-start = (bf16[512,2048]{1,0:T(8,128)(2,1)}, bf16[512,2048]{1,0:T(8,128)(2,1)}, u32[]{:S(2)}, u32[]{:S(2)}) collective-permute-start(bf16[512,2048]{1,0:T(8,128)(2,1)} %slice.117), channel_id=1, source_target_pairs={{0,1},{1,2},{2,3},{3,4},{4,5},{5,6},{6,7},{7,8},{8,9},{9,10},{10,1... | collective-permute-start | bytes 6291464 | tf_op jit(solution)/shard_map/ppermute | solution.py:14
  84.1 65.8 %collective-permute-start.2 = (bf16[512,2048]{1,0:T(8,128)(2,1)}, bf16[512,2048]{1,0:T(8,128)(2,1)S(1)}, u32[]{:S(2)}, u32[]{:S(2)}) collective-permute-start(bf16[512,2048]{1,0:T(8,128)(2,1)} %slice.117), channel_id=1, source_target_pairs={{0,15},{1,0},{2,1},{3,2},{4,3},{5,4},{6,5},{7,6},{8,7},{9,8},{10,9... | collective-permute-start | bytes 6291464 | tf_op jit(solution)/shard_map/ppermute | solution.py:14
  84.2 52.7 %collective-permute-start.4 = (s32[3,512]{1,0:T(4,128)S(1)}, s32[3,512]{1,0:T(4,128)S(1)}, u32[]{:S(2)}, u32[]{:S(2)}) collective-permute-start(s32[3,512]{1,0:T(4,128)S(1)} %pad_add_fusion), channel_id=1, source_target_pairs={{0,1},{1,2},{2,3},{3,4},{4,5},{5,6},{6,7},{7,8},{8,9},{9,10},{10,1... | collective-permute-start | bytes 18440 | tf_op jit(solution)/shard_map/ppermute | solution.py:14
  85.9 54.0 %collective-permute-start.6 = (s32[3,512]{1,0:T(4,128)S(1)}, s32[3,512]{1,0:T(4,128)S(1)}, u32[]{:S(2)}, u32[]{:S(2)}) collective-permute-start(s32[3,512]{1,0:T(4,128)S(1)} %pad_add_fusion), channel_id=1, source_target_pairs={{0,15},{1,0},{2,1},{3,2},{4,3},{5,4},{6,5},{7,6},{8,7},{9,8},{10,9... | collective-permute-start | bytes 18440 | tf_op jit(solution)/shard_map/ppermute | solution.py:14
  137.0 4.7 collective-permute-start.5
  139.9 4.3 collective-permute-start.7
  139.9 47.5 %collective-permute-start.1 = (bf16[512,2048]{1,0:T(8,128)(2,1)}, bf16[512,2048]{1,0:T(8,128)(2,1)}, u32[]{:S(2)}, u32[]{:S(2)}) collective-permute-start(bf16[512,2048]{1,0:T(8,128)(2,1)} %collective-permute-done), channel_id=1, source_target_pairs={{0,1},{1,2},{2,3},{3,4},{4,5},{5,6},{6,7},{7,8},{8,9},{9,10},{10,1... | collective-permute-start | bytes 6291464 | tf_op jit(solution)/shard_map/ppermute | solution.py:14
  149.9 48.5 %collective-permute-start.3 = (bf16[512,2048]{1,0:T(8,128)(2,1)S(1)}, bf16[512,2048]{1,0:T(8,128)(2,1)}, u32[]{:S(2)}, u32[]{:S(2)}) collective-permute-start(bf16[512,2048]{1,0:T(8,128)(2,1)S(1)} %collective-permute-done.2), channel_id=1, source_target_pairs={{0,15},{1,0},{2,1},{3,2},{4,3},{5,4},{6,5},{7,6},{8,7},{9,8},{10,9... | collective-permute-start | bytes 6291464 | tf_op jit(solution)/shard_map/ppermute | solution.py:14
  210.9 8.0 %copy-start.5 = (bf16[512,1024]{0,1:T(8,128)(2,1)S(1)}, bf16[512,1024]{0,1:T(8,128)(2,1)}, u32[]{:S(2)}) copy-start(bf16[512,1024]{0,1:T(8,128)(2,1)} %copy.21) | copy-start | bytes 3145732
  218.9 10.1 %copy-start.3 = (bf16[2560,1024]{0,1:T(8,128)(2,1)S(1)}, bf16[2560,1024]{0,1:T(8,128)(2,1)}, u32[]{:S(2)}) copy-start(bf16[2560,1024]{0,1:T(8,128)(2,1)} %copy.22) | copy-start | bytes 15728644
  255.1 7.9 %copy-start.4 = (pred[512,2560]{1,0:T(8,128)(4,1)S(1)}, pred[512,2560]{1,0:T(8,128)(4,1)}, u32[]{:S(2)}) copy-start(pred[512,2560]{1,0:T(8,128)(4,1)} %fusion.41) | copy-start | bytes 3932164
  416.5 29.5 %copy-start.10 = (f32[4]{0:T(128)S(1)}, f32[4]{0:T(128)}, u32[]{:S(2)}) copy-start(f32[4]{0:T(128)} %get-tuple-element.10) | copy-start | bytes 52
  416.5 29.5 %copy-start.11 = (f32[4]{0:T(128)S(1)}, f32[4]{0:T(128)}, u32[]{:S(2)}) copy-start(f32[4]{0:T(128)} %get-tuple-element.15) | copy-start | bytes 52
  477.6 33.9 %copy-start.1 = (bf16[512,1024]{1,0:T(8,128)(2,1)S(1)}, bf16[512,1024]{1,0:T(8,128)(2,1)}, u32[]{:S(2)}) copy-start(bf16[512,1024]{1,0:T(8,128)(2,1)} %param.7) | copy-start | bytes 3145732
Sparse Core Ops, SparseCore 0:
  9.6 64.3 all-gather.2
  88.7 55.8 all-gather.4
where the time goes:
time: 523 us; the launch traced here: 519 us
  matrix products  165 us (32%)
  waiting for transfers between devices  151 us (29%)
  other arithmetic  133 us (25%)
  local copies, waits for them, and re-layouts  45.9 us (9%)
  between operations  13.9 us (3%)
  starting transfers between devices  9.53 us (2%)
    sub x4, other arithmetic, local(): weight = jnp.where(allowed[None, :, :], jnp.exp(score - peak), 0.0)  126 us
    dot_general x4, matrix products, local(): jnp.einsum('hqk,khe->qhe', weight_bf, v_grp, preferred_element_type=jnp.f...  119 us
    ppermute x8, waiting for transfers between devices, passed_along(): lax.ppermute(value, axis, [(i, (i + by) % devices) for i in range(devices)])  83.3 us
    all_gather x1, waiting for transfers between devices, local(): lax.all_gather(w_qkv, 'ctx', axis=0, tiled=True)  66.7 us
    dot_general x4, matrix products, local(): jnp.einsum('qhe,khe->hqk', q_grp, k_grp, preferred_element_type=jnp.float32)  36.2 us
    slice x2, local copies, waits for them, and re-layouts, local(): key_heads = win_kv[:, :width].reshape(span, heads, hsize)  17.3 us
    unnamed x31, local copies, waits for them, and re-layouts  12.8 us
  transfers between devices with their start and end apart: 10, of which 5 were waited for; matrix products, arithmetic and copies ran while one was open for 64% of the time, Pallas kernels for 0%

commit v1 on v0

--- a/solution.py
+++ b/solution.py
@@ -1,8 +1,46 @@
+import functools
 import math
 import jax
 import jax.numpy as jnp
 from jax import lax
 from jax.sharding import PartitionSpec as P
+
+
+def compute_entries(frame_in, on_dim):
+    frame_in = jnp.moveaxis(frame_in, 0, on_dim)
+    even = frame_in.shape
+    local_part = frame_in.reshape(
+        *even[:on_dim], even[on_dim] * even[on_dim + 1], *even[on_dim + 2 :]
+    )
+    return local_part
+
+
+def shape_lots_all(here_x, axis_id, dim_no):
+    chips = lax.axis_size(axis_id)
+    table = []
+    for m in range(chips):
+        table.append((m, (m + 1) % chips))
+    block_list = []
+    for tick, to_i in table:
+        block_list.append((to_i, tick))
+    earlier, z_new = ([], [])
+    for nth in range(chips - 1):
+        if nth % 2 == 0:
+            n_now = lax.ppermute(earlier[-1] if earlier else here_x, axis_name=axis_id, perm=table)
+            earlier.append(n_now)
+        else:
+            raw_out = lax.ppermute(z_new[-1] if z_new else here_x, axis_id, block_list)
+            z_new.append(raw_out)
+    after = jnp.stack([*earlier[::-1], here_x, *z_new], axis=0)
+    taken_in = lax.axis_index(axis_id)
+    state_next = len(earlier)
+    now = taken_in - state_next
+    after = after[(jnp.arange(chips) - now) % chips]
+    b_next = compute_entries(after, dim_no)
+    return b_next
+
+
+reach_pages_on = functools.partial(shape_lots_all, axis_id="ctx", dim_no=0)
 
 
 def as_sent(value):
@@ -35,11 +73,7 @@
     center = lax.axis_index("ctx")
     count = lax.axis_size("ctx")
     columns = tokens
-    qkv = jnp.dot(
-        columns,
-        lax.all_gather(w_qkv, "ctx", axis=0, tiled=True),
-        preferred_element_type=jnp.float32,
-    )
+    qkv = jnp.dot(columns, reach_pages_on(w_qkv), preferred_element_type=jnp.float32)
     qkv = qkv.astype(jnp.bfloat16)
     query = qkv[:, :width]
     keyval = qkv[:, width:]

time: 523 us -> 548 us (1.048)
  starting transfers between devices: 9.53 us -> 29.9 us
    all_gather x1 -> x0, waiting for transfers between devices: 66.7 us -> none  [local(): lax.all_gather(w_qkv, 'ctx', axis=0, tiled=True)]
    ppermute x0 -> x15, waiting for transfers between devices: none -> 59 us  [the longest x8 57.2 us: shape_lots_all(): lax.ppermute(earlier[-1] if earlier else here_x, axis_name=axis_id, perm=...]
    ppermute x0 -> x15, starting transfers between devices: none -> 21.2 us  [the longest x8 20 us: shape_lots_all(): lax.ppermute(earlier[-1] if earlier else here_x, axis_name=axis_id, perm=...]
    unnamed x31 -> x62, local copies, waits for them, and re-layouts: 12.8 us -> 30 us
    slice x2 -> x1, local copies, waits for them, and re-layouts: 17.3 us -> 8.62 us  [local(): key_heads = win_kv[:, :width].reshape(span, heads, hsize)]
    slice x1 -> x0, local copies, waits for them, and re-layouts: 7.89 us -> none  [local(): value_heads = win_kv[:, width:].reshape(span, heads, hsize)]
    gather x0 -> x1, local copies, waits for them, and re-layouts: none -> 6.38 us  [shape_lots_all(): after = after[(jnp.arange(chips) - now) % chips]]
  transfers between devices with their start and end apart: 10 -> 24, of which waited for: 5 -> 17; matrix products, arithmetic and copies ran while one was open for 64% -> 61% of each run, Pallas kernels for 0% -> 0%
where the time goes in v1:
time: 548 us; the launch traced here: 540 us
  matrix products  166 us (30%)
  waiting for transfers between devices  146 us (27%)
  other arithmetic  133 us (24%)
  local copies, waits for them, and re-layouts  50.7 us (9%)
  starting transfers between devices  29.9 us (5%)
  between operations  13.9 us (3%)
    sub x4, other arithmetic, local(): weight = jnp.where(allowed[None, :, :], jnp.exp(score - peak), 0.0)  126 us
    dot_general x4, matrix products, local(): jnp.einsum('hqk,khe->qhe', weight_bf, v_grp, preferred_element_type=jnp.f...  119 us
    ppermute x8, waiting for transfers between devices, passed_along(): lax.ppermute(value, axis, [(i, (i + by) % devices) for i in range(devices)])  86.6 us
    ppermute x8, waiting for transfers between devices, shape_lots_all(): lax.ppermute(earlier[-1] if earlier else here_x, axis_name=axis_id, perm=...  57.2 us
    dot_general x4, matrix products, local(): jnp.einsum('qhe,khe->hqk', q_grp, k_grp, preferred_element_type=jnp.float32)  36.8 us
    unnamed x62, local copies, waits for them, and re-layouts  30 us
    ppermute x8, starting transfers between devices, shape_lots_all(): lax.ppermute(earlier[-1] if earlier else here_x, axis_name=axis_id, perm=...  20 us
  transfers between devices with their start and end apart: 24, of which 17 were waited for; matrix products, arithmetic and copies ran while one was open for 61% of the time, Pallas kernels for 0%

profile of v1, /device:TPU:1, one launch (start us, length us, event | category | flops | bytes accessed | tf_op | source)
XLA Modules:
  0.0 539.7 jit_solution(9626187341493043082)
XLA Ops:
  6.5 2.6 collective-permute-start
  9.2 5.0 collective-permute-done
  14.2 2.4 collective-permute-start.1
  17.7 7.8 %collective-permute-done.1 = bf16[64,3072]{1,0:T(8,128)(2,1)S(1)} collective-permute-done((bf16[64,3072]{1,0:T(8,128)(2,1)S(1)}, bf16[64,3072]{1,0:T(8,128)(2,1)S(1)}, u32[]{:S(2)}, u32[]{:S(2)}) %collective-permute-start.1) | collective-permute-done | bytes 393248 | tf_op jit(solution)/shard_map/ppermute | solution.py:29
  25.5 2.5 collective-permute-start.2
  28.2 8.7 %collective-permute-done.2 = bf16[64,3072]{1,0:T(8,128)(2,1)S(1)} collective-permute-done((bf16[64,3072]{1,0:T(8,128)(2,1)S(1)}, bf16[64,3072]{1,0:T(8,128)(2,1)S(1)}, u32[]{:S(2)}, u32[]{:S(2)}) %collective-permute-start.2) | collective-permute-done | bytes 393248 | tf_op jit(solution)/shard_map/ppermute | solution.py:29
  36.9 2.5 collective-permute-start.3
  39.6 8.0 %collective-permute-done.3 = bf16[64,3072]{1,0:T(8,128)(2,1)S(1)} collective-permute-done((bf16[64,3072]{1,0:T(8,128)(2,1)S(1)}, bf16[64,3072]{1,0:T(8,128)(2,1)S(1)}, u32[]{:S(2)}, u32[]{:S(2)}) %collective-permute-start.3) | collective-permute-done | bytes 393248 | tf_op jit(solution)/shard_map/ppermute | solution.py:29
  47.6 2.5 collective-permute-start.4
  51.8 7.2 %collective-permute-done.4 = bf16[64,3072]{1,0:T(8,128)(2,1)S(1)} collective-permute-done((bf16[64,3072]{1,0:T(8,128)(2,1)S(1)}, bf16[64,3072]{1,0:T(8,128)(2,1)S(1)}, u32[]{:S(2)}, u32[]{:S(2)}) %collective-permute-start.4) | collective-permute-done | bytes 393248 | tf_op jit(solution)/shard_map/ppermute | solution.py:29
  59.0 2.5 collective-permute-start.5
  62.2 6.3 %collective-permute-done.5 = bf16[64,3072]{1,0:T(8,128)(2,1)S(1)} collective-permute-done((bf16[64,3072]{1,0:T(8,128)(2,1)S(1)}, bf16[64,3072]{1,0:T(8,128)(2,1)S(1)}, u32[]{:S(2)}, u32[]{:S(2)}) %collective-permute-start.5) | collective-permute-done | bytes 393248 | tf_op jit(solution)/shard_map/ppermute | solution.py:29
  68.5 2.5 collective-permute-start.6
  71.3 7.3 %collective-permute-done.6 = bf16[64,3072]{1,0:T(8,128)(2,1)} collective-permute-done((bf16[64,3072]{1,0:T(8,128)(2,1)S(1)}, bf16[64,3072]{1,0:T(8,128)(2,1)}, u32[]{:S(2)}, u32[]{:S(2)}) %collective-permute-start.6) | collective-permute-done | bytes 393248 | tf_op jit(solution)/shard_map/ppermute | solution.py:29
  78.6 2.6 collective-permute-start.7
  81.3 6.9 %collective-permute-done.7 = bf16[64,3072]{1,0:T(8,128)(2,1)} collective-permute-done((bf16[64,3072]{1,0:T(8,128)(2,1)}, bf16[64,3072]{1,0:T(8,128)(2,1)}, u32[]{:S(2)}, u32[]{:S(2)}) %collective-permute-start.7) | collective-permute-done | bytes 393248 | tf_op jit(solution)/shard_map/ppermute | solution.py:29
  88.2 1.8 bitcast_dynamic-update-slice_fusion.15
  90.0 1.8 bitcast_dynamic-update-slice_fusion.14
  91.8 1.8 bitcast_dynamic-update-slice_fusion.13
  93.5 1.8 bitcast_dynamic-update-slice_fusion.12
  95.3 1.8 bitcast_dynamic-update-slice_fusion.11
  103.4 1.8 bitcast_dynamic-update-slice_fusion.2
  105.2 1.8 bitcast_dynamic-update-slice_fusion.1
  107.7 6.4 %gather_fusion = bf16[16,64,3072]{2,1,0:T(8,128)(2,1)} fusion(bf16[16,64,3072]{2,1,0:T(8,128)(2,1)} %bitcast_dynamic-update-slice_fusion, s32[1024]{0:T(1024)S(1)} %pad_clamp_fusion), kind=kCustom, calls=%fused_computation | custom fusion | bytes 12582976 | tf_op jit(solution)/shard_map/gather | solution.py:38
  114.1 6.6 %fusion.42 = bf16[512,3072]{0,1:T(8,128)(2,1)S(1)} fusion(bf16[1024,3072]{1,0:T(8,128)(2,1)} %bitcast.100, bf16[512,1024]{1,0:T(8,128)(2,1)S(1)} %copy-done), kind=kOutput, calls=%fused_computation.53 | convolution fusion | flops 3222798336 | bytes 10485760 | tf_op jit(solution)/shard_map/dot_general | solution.py:76
  124.0 2.5 collective-permute-start.15
  126.5 1.8 collective-permute-start.19
  129.3 48.0 %collective-permute-done.19 = s32[3,512]{1,0:T(4,128)S(1)} collective-permute-done((s32[3,512]{1,0:T(4,128)S(1)}, s32[3,512]{1,0:T(4,128)S(1)}, u32[]{:S(2)}, u32[]{:S(2)}) %collective-permute-start.19) | collective-permute-done | bytes 6176 | tf_op jit(solution)/shard_map/ppermute | solution.py:52
  177.3 2.5 collective-permute-start.20
  183.2 2.4 collective-permute-done.22
  185.7 5.5 %fusion.41 = pred[512,2560]{1,0:T(8,128)(4,1)} fusion(s32[2560]{0:T(1024)S(1)} %iota_add_fusion, s32[512]{0:T(512)S(1)} %iota_add_fusion.1, s32[2560]{0:T(1024)S(1)} %get-tuple-element.7, s32[2560]{0:T(1024)S(1)} %get-tuple-element.5, s32[512]{0:T(512)S(1)} %copy-done.14, s32[512]{0:T(512)S(1)} %copy-done.15, pred[2560]{0:T(1024)(128)(4,1)S(1)} %compare_and_fusion), kind=kLoop, calls=%fused_computation.51 | loop fusion | flops 10485760 | bytes 1350144 | tf_op jit(solution)/shard_map/and | solution.py:90
  191.2 1.9 broadcast_compare_fusion
  194.4 34.5 %collective-permute-done.16 = bf16[512,2048]{0,1:T(8,128)(2,1)S(1)} collective-permute-done((bf16[512,2048]{0,1:T(8,128)(2,1)}, bf16[512,2048]{0,1:T(8,128)(2,1)S(1)}, u32[]{:S(2)}, u32[]{:S(2)}) %collective-permute-start.16) | collective-permute-done | bytes 2097184 | tf_op jit(solution)/shard_map/ppermute | solution.py:52
  230.5 3.1 constant_dynamic-update-slice_fusion.3
  238.4 8.6 %fusion.121 = (bf16[2560,1024]{0,1:T(8,128)(2,1)}, bf16[2560,1024]{0,1:T(8,128)(2,1)}) fusion(bf16[2560,2048]{0,1:T(8,128)(2,1)} %constant_dynamic-update-slice_fusion), kind=kLoop, calls=%fused_computation.149 | loop fusion | bytes 20971520 | tf_op jit(solution)/shard_map/slice | solution.py:93
  247.0 10.6 %fusion.49 = f32[4,512,2560]{2,1,0:T(8,128)} fusion(bf16[512,16,64]{0,2,1:T(8,128)(2,1)S(1)} %bitcast.110, bf16[2560,16,64]{0,2,1:T(8,128)(2,1)} %bitcast.105), kind=kOutput, calls=%fused_computation.62 | convolution fusion | flops 671088640 | bytes 23330816 | tf_op jit(solution)/shard_map/qhe,khe->hqk/dot_general | solution.py:108
  257.6 8.6 %fusion.47 = f32[4,512,2560]{2,1,0:T(8,128)} fusion(bf16[512,16,64]{0,2,1:T(8,128)(2,1)S(1)} %bitcast.111, bf16[2560,16,64]{0,2,1:T(8,128)(2,1)S(1)} %bitcast.106), kind=kOutput, calls=%fused_computation.60 | convolution fusion | flops 671088640 | bytes 23330816 | tf_op jit(solution)/shard_map/qhe,khe->hqk/dot_general | solution.py:108
  266.3 8.8 %fusion.45 = f32[4,512,2560]{2,1,0:T(8,128)} fusion(bf16[512,16,64]{0,2,1:T(8,128)(2,1)S(1)} %bitcast.112, bf16[2560,16,64]{0,2,1:T(8,128)(2,1)S(1)} %bitcast.107), kind=kOutput, calls=%fused_computation.58 | convolution fusion | flops 671088640 | bytes 23330816 | tf_op jit(solution)/shard_map/qhe,khe->hqk/dot_general | solution.py:108
  275.1 8.7 %fusion.43 = f32[4,512,2560]{2,1,0:T(8,128)} fusion(bf16[512,16,64]{0,2,1:T(8,128)(2,1)S(1)} %bitcast.113, bf16[2560,16,64]{0,2,1:T(8,128)(2,1)S(1)} %bitcast.108), kind=kOutput, calls=%fused_computation.56 | convolution fusion | flops 671088640 | bytes 23330816 | tf_op jit(solution)/shard_map/qhe,khe->hqk/dot_general | solution.py:108
  283.8 31.2 %fusion.125 = f32[4,512]{1,0:T(4,128)S(1)} fusion(f32[4,512,2560]{2,1,0:T(8,128)} %fusion.49, f32[4]{0:T(128)S(1)} %get-tuple-element.15, f32[4]{0:T(128)S(1)} %get-tuple-element.10, pred[512,2560]{1,0:T(8,128)(4,1)} %broadcast_compare_fusion, pred[512,2560]{1,0:T(8,128)(4,1)S(1)} %copy-done.5), kind=kOutput, calls=%fused_computation.153 | output fusion | flops 36702720 | bytes 23601184 | tf_op jit(solution)/shard_map/sub | solution.py:113
  315.0 29.8 %fusion.84 = bf16[512,4,64]{0,2,1:T(8,128)(2,1)S(1)} fusion(bf16[2560,16,64]{0,2,1:T(8,128)(2,1)} %bitcast.101, f32[4,512,2560]{2,1,0:T(8,128)} %fusion.49, f32[4]{0:T(128)S(1)} %get-tuple-element.15, f32[4]{0:T(128)S(1)} %get-tuple-element.10, pred[512,2560]{1,0:T(8,128)(4,1)} %broadcast_compare_fusion, pred[512,2560]{1,0:T(8,128)(4,1)S(1)} %copy-done.5, ...), kind=kOutput, calls=%fused_computation.76 | convolution fusion | flops 708055552 | bytes 29106208 | tf_op jit(solution)/shard_map/hqk,khe->qhe/dot_general | solution.py:116
  344.8 31.6 %fusion.124 = f32[4,512]{1,0:T(4,128)S(1)} fusion(f32[4,512,2560]{2,1,0:T(8,128)} %fusion.47, f32[4]{0:T(128)S(1)} %get-tuple-element.13, f32[4]{0:T(128)S(1)} %get-tuple-element.14, pred[512,2560]{1,0:T(8,128)(4,1)} %broadcast_compare_fusion, pred[512,2560]{1,0:T(8,128)(4,1)S(1)} %copy-done.5), kind=kOutput, calls=%fused_computation.152 | output fusion | flops 36702720 | bytes 23601184 | tf_op jit(solution)/shard_map/sub | solution.py:113
  376.4 29.5 %fusion.78 = bf16[512,4,64]{0,2,1:T(8,128)(2,1)S(1)} fusion(bf16[2560,16,64]{0,2,1:T(8,128)(2,1)} %bitcast.102, f32[4,512,2560]{2,1,0:T(8,128)} %fusion.47, f32[4]{0:T(128)S(1)} %get-tuple-element.13, f32[4]{0:T(128)S(1)} %get-tuple-element.14, pred[512,2560]{1,0:T(8,128)(4,1)} %broadcast_compare_fusion, pred[512,2560]{1,0:T(8,128)(4,1)S(1)} %copy-done.5, ...), kind=kOutput, calls=%fused_computation.74 | convolution fusion | flops 708055552 | bytes 29106208 | tf_op jit(solution)/shard_map/hqk,khe->qhe/dot_general | solution.py:116
  405.9 31.3 %fusion.123 = f32[4,512]{1,0:T(4,128)S(1)} fusion(f32[4,512,2560]{2,1,0:T(8,128)} %fusion.45, f32[4]{0:T(128)S(1)} %get-tuple-element.11, f32[4]{0:T(128)S(1)} %get-tuple-element.12, pred[512,2560]{1,0:T(8,128)(4,1)} %broadcast_compare_fusion, pred[512,2560]{1,0:T(8,128)(4,1)S(1)} %copy-done.5), kind=kOutput, calls=%fused_computation.151 | output fusion | flops 36702720 | bytes 23601184 | tf_op jit(solution)/shard_map/sub | solution.py:113
  437.3 29.9 %fusion.72 = bf16[512,4,64]{0,2,1:T(8,128)(2,1)S(1)} fusion(bf16[2560,16,64]{0,2,1:T(8,128)(2,1)} %bitcast.103, f32[4,512,2560]{2,1,0:T(8,128)} %fusion.45, f32[4]{0:T(128)S(1)} %get-tuple-element.11, f32[4]{0:T(128)S(1)} %get-tuple-element.12, pred[512,2560]{1,0:T(8,128)(4,1)} %broadcast_compare_fusion, pred[512,2560]{1,0:T(8,128)(4,1)S(1)} %copy-done.5, ...), kind=kOutput, calls=%fused_computation.72 | convolution fusion | flops 708055552 | bytes 29106208 | tf_op jit(solution)/shard_map/hqk,khe->qhe/dot_general | solution.py:116
  467.2 31.5 %fusion.122 = f32[4,512]{1,0:T(4,128)S(1)} fusion(f32[4,512,2560]{2,1,0:T(8,128)} %fusion.43, f32[4]{0:T(128)S(1)} %copy-done.18, f32[4]{0:T(128)S(1)} %copy-done.19, pred[512,2560]{1,0:T(8,128)(4,1)} %broadcast_compare_fusion, pred[512,2560]{1,0:T(8,128)(4,1)S(1)} %copy-done.5), kind=kOutput, calls=%fused_computation.150 | output fusion | flops 36702720 | bytes 23601184 | tf_op jit(solution)/shard_map/sub | solution.py:113
  498.7 29.9 %fusion.66 = bf16[512,4,64]{0,2,1:T(8,128)(2,1)S(1)} fusion(bf16[2560,16,64]{0,2,1:T(8,128)(2,1)} %bitcast.104, f32[4,512,2560]{2,1,0:T(8,128)} %fusion.43, f32[4]{0:T(128)S(1)} %copy-done.18, f32[4]{0:T(128)S(1)} %copy-done.19, pred[512,2560]{1,0:T(8,128)(4,1)} %broadcast_compare_fusion, pred[512,2560]{1,0:T(8,128)(4,1)S(1)} %copy-done.5, ...), kind=kOutput, calls=%fused_computation.70 | convolution fusion | flops 708055552 | bytes 29106208 | tf_op jit(solution)/shard_map/hqk,khe->qhe/dot_general | solution.py:116
  528.8 3.8 convolution_convert_fusion.1
  (96 shorter events, 27.0 us)
Async XLA Ops:
  6.5 107.6 %copy-start = (bf16[512,1024]{1,0:T(8,128)(2,1)S(1)}, bf16[512,1024]{1,0:T(8,128)(2,1)}, u32[]{:S(2)}) copy-start(bf16[512,1024]{1,0:T(8,128)(2,1)} %param.7) | copy-start | bytes 3145732
  6.5 92.9 %copy-start.6 = (bf16[64,3072]{1,0:T(8,128)(2,1)S(1)}, bf16[64,3072]{1,0:T(8,128)(2,1)}, u32[]{:S(2)}) copy-start(bf16[64,3072]{1,0:T(8,128)(2,1)} %param.8) | copy-start | bytes 1179652
  6.5 522.2 %all-gather.2.cloned.1.call-start = ((), (), s32[]{:S(2)}) async-start(), calls=%async_computation | async-start | bytes 2228224 | tf_op jit(solution)/shard_map/all_gather | solution.py:122
  6.5 7.7 %collective-permute-start = (bf16[64,3072]{1,0:T(8,128)(2,1)}, bf16[64,3072]{1,0:T(8,128)(2,1)S(1)}, u32[]{:S(2)}, u32[]{:S(2)}) collective-permute-start(bf16[64,3072]{1,0:T(8,128)(2,1)} %param.8), channel_id=1, source_target_pairs={{0,1},{1,2},{2,3},{3,4},{4,5},{5,6},{6,7},{7,8},{8,9},{9,10},{10,1... | collective-permute-start | bytes 1179656 | tf_op jit(solution)/shard_map/ppermute | solution.py:29
  14.2 11.3 %collective-permute-start.1 = (bf16[64,3072]{1,0:T(8,128)(2,1)S(1)}, bf16[64,3072]{1,0:T(8,128)(2,1)S(1)}, u32[]{:S(2)}, u32[]{:S(2)}) collective-permute-start(bf16[64,3072]{1,0:T(8,128)(2,1)S(1)} %collective-permute-done), channel_id=1, source_target_pairs={{0,1},{1,2},{2,3},{3,4},{4,5},{5,6},{6,7},{7,8},{8,9},{9,10},{10,1... | collective-permute-start | bytes 1179656 | tf_op jit(solution)/shard_map/ppermute | solution.py:29
  16.6 11.6 %collective-permute-start.8 = (bf16[64,3072]{1,0:T(8,128)(2,1)}, bf16[64,3072]{1,0:T(8,128)(2,1)S(1)}, u32[]{:S(2)}, u32[]{:S(2)}) collective-permute-start(bf16[64,3072]{1,0:T(8,128)(2,1)} %param.8), channel_id=1, source_target_pairs={{1,0},{2,1},{3,2},{4,3},{5,4},{6,5},{7,6},{8,7},{9,8},{10,9},{11,1... | collective-permute-start | bytes 1179656 | tf_op jit(solution)/shard_map/ppermute | solution.py:32
  25.5 11.4 %collective-permute-start.2 = (bf16[64,3072]{1,0:T(8,128)(2,1)S(1)}, bf16[64,3072]{1,0:T(8,128)(2,1)S(1)}, u32[]{:S(2)}, u32[]{:S(2)}) collective-permute-start(bf16[64,3072]{1,0:T(8,128)(2,1)S(1)} %collective-permute-done.1), channel_id=1, source_target_pairs={{0,1},{1,2},{2,3},{3,4},{4,5},{5,6},{6,7},{7,8},{8,9},{9,10},{10,1... | collective-permute-start | bytes 1179656 | tf_op jit(solution)/shard_map/ppermute | solution.py:29
  28.2 11.4 %collective-permute-start.9 = (bf16[64,3072]{1,0:T(8,128)(2,1)S(1)}, bf16[64,3072]{1,0:T(8,128)(2,1)S(1)}, u32[]{:S(2)}, u32[]{:S(2)}) collective-permute-start(bf16[64,3072]{1,0:T(8,128)(2,1)S(1)} %collective-permute-done.8), channel_id=1, source_target_pairs={{1,0},{2,1},{3,2},{4,3},{5,4},{6,5},{7,6},{8,7},{9,8},{10,9},{11,1... | collective-permute-start | bytes 1179656 | tf_op jit(solution)/shard_map/ppermute | solution.py:32
  36.9 10.6 %collective-permute-start.3 = (bf16[64,3072]{1,0:T(8,128)(2,1)S(1)}, bf16[64,3072]{1,0:T(8,128)(2,1)S(1)}, u32[]{:S(2)}, u32[]{:S(2)}) collective-permute-start(bf16[64,3072]{1,0:T(8,128)(2,1)S(1)} %collective-permute-done.2), channel_id=1, source_target_pairs={{0,1},{1,2},{2,3},{3,4},{4,5},{5,6},{6,7},{7,8},{8,9},{9,10},{10,1... | collective-permute-start | bytes 1179656 | tf_op jit(solution)/shard_map/ppermute | solution.py:29
  39.6 11.4 %collective-permute-start.10 = (bf16[64,3072]{1,0:T(8,128)(2,1)S(1)}, bf16[64,3072]{1,0:T(8,128)(2,1)S(1)}, u32[]{:S(2)}, u32[]{:S(2)}) collective-permute-start(bf16[64,3072]{1,0:T(8,128)(2,1)S(1)} %collective-permute-done.9), channel_id=1, source_target_pairs={{1,0},{2,1},{3,2},{4,3},{5,4},{6,5},{7,6},{8,7},{9,8},{10,9},{11,1... | collective-permute-start | bytes 1179656 | tf_op jit(solution)/shard_map/ppermute | solution.py:32
  47.6 23.7 %copy-start.11 = (bf16[64,3072]{1,0:T(8,128)(2,1)}, bf16[64,3072]{1,0:T(8,128)(2,1)S(1)}, u32[]{:S(2)}) copy-start(bf16[64,3072]{1,0:T(8,128)(2,1)S(1)} %collective-permute-done.3) | copy-start | bytes 1179652
  47.6 11.4 %collective-permute-start.4 = (bf16[64,3072]{1,0:T(8,128)(2,1)S(1)}, bf16[64,3072]{1,0:T(8,128)(2,1)S(1)}, u32[]{:S(2)}, u32[]{:S(2)}) collective-permute-start(bf16[64,3072]{1,0:T(8,128)(2,1)S(1)} %collective-permute-done.3), channel_id=1, source_target_pairs={{0,1},{1,2},{2,3},{3,4},{4,5},{5,6},{6,7},{7,8},{8,9},{9,10},{10,1... | collective-permute-start | bytes 1179656 | tf_op jit(solution)/shard_map/ppermute | solution.py:29
  51.0 0.7 copy-start.7
  51.8 9.7 %collective-permute-start.11 = (bf16[64,3072]{1,0:T(8,128)(2,1)S(1)}, bf16[64,3072]{1,0:T(8,128)(2,1)S(1)}, u32[]{:S(2)}, u32[]{:S(2)}) collective-permute-start(bf16[64,3072]{1,0:T(8,128)(2,1)S(1)} %collective-permute-done.10), channel_id=1, source_target_pairs={{1,0},{2,1},{3,2},{4,3},{5,4},{6,5},{7,6},{8,7},{9,8},{10,9},{11,1... | collective-permute-start | bytes 1179656 | tf_op jit(solution)/shard_map/ppermute | solution.py:32
  59.0 12.3 %copy-start.12 = (bf16[64,3072]{1,0:T(8,128)(2,1)}, bf16[64,3072]{1,0:T(8,128)(2,1)S(1)}, u32[]{:S(2)}) copy-start(bf16[64,3072]{1,0:T(8,128)(2,1)S(1)} %collective-permute-done.4) | copy-start | bytes 1179652
  59.0 9.6 %collective-permute-start.5 = (bf16[64,3072]{1,0:T(8,128)(2,1)S(1)}, bf16[64,3072]{1,0:T(8,128)(2,1)S(1)}, u32[]{:S(2)}, u32[]{:S(2)}) collective-permute-start(bf16[64,3072]{1,0:T(8,128)(2,1)S(1)} %collective-permute-done.4), channel_id=1, source_target_pairs={{0,1},{1,2},{2,3},{3,4},{4,5},{5,6},{6,7},{7,8},{8,9},{9,10},{10,1... | collective-permute-start | bytes 1179656 | tf_op jit(solution)/shard_map/ppermute | solution.py:29
  61.5 0.7 copy-start.9
  62.2 9.1 %collective-permute-start.12 = (bf16[64,3072]{1,0:T(8,128)(2,1)S(1)}, bf16[64,3072]{1,0:T(8,128)(2,1)}, u32[]{:S(2)}, u32[]{:S(2)}) collective-permute-start(bf16[64,3072]{1,0:T(8,128)(2,1)S(1)} %collective-permute-done.11), channel_id=1, source_target_pairs={{1,0},{2,1},{3,2},{4,3},{5,4},{6,5},{7,6},{8,7},{9,8},{10,9},{11,1... | collective-permute-start | bytes 1179656 | tf_op jit(solution)/shard_map/ppermute | solution.py:32
  68.5 10.1 %copy-start.13 = (bf16[64,3072]{1,0:T(8,128)(2,1)}, bf16[64,3072]{1,0:T(8,128)(2,1)S(1)}, u32[]{:S(2)}) copy-start(bf16[64,3072]{1,0:T(8,128)(2,1)S(1)} %collective-permute-done.5) | copy-start | bytes 1179652
  68.5 10.0 %collective-permute-start.6 = (bf16[64,3072]{1,0:T(8,128)(2,1)S(1)}, bf16[64,3072]{1,0:T(8,128)(2,1)}, u32[]{:S(2)}, u32[]{:S(2)}) collective-permute-start(bf16[64,3072]{1,0:T(8,128)(2,1)S(1)} %collective-permute-done.5), channel_id=1, source_target_pairs={{0,1},{1,2},{2,3},{3,4},{4,5},{5,6},{6,7},{7,8},{8,9},{9,10},{10,1... | collective-permute-start | bytes 1179656 | tf_op jit(solution)/shard_map/ppermute | solution.py:29
  71.3 10.0 %collective-permute-start.13 = (bf16[64,3072]{1,0:T(8,128)(2,1)}, bf16[64,3072]{1,0:T(8,128)(2,1)}, u32[]{:S(2)}, u32[]{:S(2)}) collective-permute-start(bf16[64,3072]{1,0:T(8,128)(2,1)} %collective-permute-done.12), channel_id=1, source_target_pairs={{1,0},{2,1},{3,2},{4,3},{5,4},{6,5},{7,6},{8,7},{9,8},{10,9},{11,1... | collective-permute-start | bytes 1179656 | tf_op jit(solution)/shard_map/ppermute | solution.py:32
  78.6 9.6 %collective-permute-start.7 = (bf16[64,3072]{1,0:T(8,128)(2,1)}, bf16[64,3072]{1,0:T(8,128)(2,1)}, u32[]{:S(2)}, u32[]{:S(2)}) collective-permute-start(bf16[64,3072]{1,0:T(8,128)(2,1)} %collective-permute-done.6), channel_id=1, source_target_pairs={{0,1},{1,2},{2,3},{3,4},{4,5},{5,6},{6,7},{7,8},{8,9},{9,10},{10,1... | collective-permute-start | bytes 1179656 | tf_op jit(solution)/shard_map/ppermute | solution.py:29
  81.2 20.6 %copy-start.8 = (bf16[64,3072]{1,0:T(8,128)(2,1)S(1)}, bf16[64,3072]{1,0:T(8,128)(2,1)}, u32[]{:S(2)}) copy-start(bf16[64,3072]{1,0:T(8,128)(2,1)} %copy-done.7) | copy-start | bytes 1179652
  81.2 21.4 %copy-start.10 = (bf16[64,3072]{1,0:T(8,128)(2,1)S(1)}, bf16[64,3072]{1,0:T(8,128)(2,1)}, u32[]{:S(2)}) copy-start(bf16[64,3072]{1,0:T(8,128)(2,1)} %copy-done.9) | copy-start | bytes 1179652
  81.3 25.7 %collective-permute-start.14 = (bf16[64,3072]{1,0:T(8,128)(2,1)}, bf16[64,3072]{1,0:T(8,128)(2,1)S(1)}, u32[]{:S(2)}, u32[]{:S(2)}) collective-permute-start(bf16[64,3072]{1,0:T(8,128)(2,1)} %collective-permute-done.13), channel_id=1, source_target_pairs={{1,0},{2,1},{3,2},{4,3},{5,4},{6,5},{7,6},{8,7},{9,8},{10,9},{11,1... | collective-permute-start | bytes 1179656 | tf_op jit(solution)/shard_map/ppermute | solution.py:32
  114.1 12.4 %copy-start.14 = (s32[512]{0:T(512)S(1)}, s32[512]{0:T(512)}, u32[]{:S(2)}) copy-start(s32[512]{0:T(512)} %param.13) | copy-start | bytes 6148
  114.1 12.4 %copy-start.15 = (s32[512]{0:T(512)S(1)}, s32[512]{0:T(512)}, u32[]{:S(2)}) copy-start(s32[512]{0:T(512)} %param.11) | copy-start | bytes 6148
  114.1 12.4 %copy-start.16 = (s32[512]{0:T(512)S(1)}, s32[512]{0:T(512)}, u32[]{:S(2)}) copy-start(s32[512]{0:T(512)} %param.12) | copy-start | bytes 6148
  114.1 14.5 %copy-start.17 = (f32[2,16]{1,0:T(2,128)S(1)}, f32[2,16]{1,0:T(2,128)}, u32[]{:S(2)}) copy-start(f32[2,16]{1,0:T(2,128)} %param.10) | copy-start | bytes 388
  120.8 1.7 copy-start.2
  124.0 57.4 %collective-permute-start.15 = (bf16[512,2048]{0,1:T(8,128)(2,1)}, bf16[512,2048]{0,1:T(8,128)(2,1)}, u32[]{:S(2)}, u32[]{:S(2)}) collective-permute-start(bf16[512,2048]{0,1:T(8,128)(2,1)} %slice.119), channel_id=1, source_target_pairs={{0,1},{1,2},{2,3},{3,4},{4,5},{5,6},{6,7},{7,8},{8,9},{9,10},{10,1... | collective-permute-start | bytes 6291464 | tf_op jit(solution)/shard_map/ppermute | solution.py:52
  126.5 64.7 %collective-permute-start.17 = (bf16[512,2048]{0,1:T(8,128)(2,1)}, bf16[512,2048]{0,1:T(8,128)(2,1)S(1)}, u32[]{:S(2)}, u32[]{:S(2)}) collective-permute-start(bf16[512,2048]{0,1:T(8,128)(2,1)} %slice.119), channel_id=1, source_target_pairs={{0,15},{1,0},{2,1},{3,2},{4,3},{5,4},{6,5},{7,6},{8,7},{9,8},{10,9... | collective-permute-start | bytes 6291464 | tf_op jit(solution)/shard_map/ppermute | solution.py:52
  126.5 50.8 %collective-permute-start.19 = (s32[3,512]{1,0:T(4,128)S(1)}, s32[3,512]{1,0:T(4,128)S(1)}, u32[]{:S(2)}, u32[]{:S(2)}) collective-permute-start(s32[3,512]{1,0:T(4,128)S(1)} %pad_add_fusion), channel_id=1, source_target_pairs={{0,1},{1,2},{2,3},{3,4},{4,5},{5,6},{6,7},{7,8},{8,9},{9,10},{10,1... | collective-permute-start | bytes 18440 | tf_op jit(solution)/shard_map/ppermute | solution.py:52
  128.3 53.1 %collective-permute-start.21 = (s32[3,512]{1,0:T(4,128)S(1)}, s32[3,512]{1,0:T(4,128)S(1)}, u32[]{:S(2)}, u32[]{:S(2)}) collective-permute-start(s32[3,512]{1,0:T(4,128)S(1)} %pad_add_fusion), channel_id=1, source_target_pairs={{0,15},{1,0},{2,1},{3,2},{4,3},{5,4},{6,5},{7,6},{8,7},{9,8},{10,9... | collective-permute-start | bytes 18440 | tf_op jit(solution)/shard_map/ppermute | solution.py:52
  177.3 5.9 %collective-permute-start.20 = (s32[3,512]{1,0:T(4,128)S(1)}, s32[3,512]{1,0:T(4,128)S(1)}, u32[]{:S(2)}, u32[]{:S(2)}) collective-permute-start(s32[3,512]{1,0:T(4,128)S(1)} %collective-permute-done.19), channel_id=1, source_target_pairs={{0,1},{1,2},{2,3},{3,4},{4,5},{5,6},{6,7},{7,8},{8,9},{9,10},{10,1... | collective-permute-start | bytes 18440 | tf_op jit(solution)/shard_map/ppermute | solution.py:52
  181.4 4.2 collective-permute-start.22
  181.4 47.5 %collective-permute-start.16 = (bf16[512,2048]{0,1:T(8,128)(2,1)}, bf16[512,2048]{0,1:T(8,128)(2,1)S(1)}, u32[]{:S(2)}, u32[]{:S(2)}) collective-permute-start(bf16[512,2048]{0,1:T(8,128)(2,1)} %collective-permute-done.15), channel_id=1, source_target_pairs={{0,1},{1,2},{2,3},{3,4},{4,5},{5,6},{6,7},{7,8},{8,9},{9,10},{10,1... | collective-permute-start | bytes 6291464 | tf_op jit(solution)/shard_map/ppermute | solution.py:52
  185.7 48.0 %copy-start.3 = (bf16[512,3072]{0,1:T(8,128)(2,1)S(1)}, bf16[512,3072]{0,1:T(8,128)(2,1)}, u32[]{:S(2)}) copy-start(bf16[512,3072]{0,1:T(8,128)(2,1)} %copy-done.2) | copy-start | bytes 9437188
  191.2 45.6 %collective-permute-start.18 = (bf16[512,2048]{0,1:T(8,128)(2,1)S(1)}, bf16[512,2048]{0,1:T(8,128)(2,1)S(1)}, u32[]{:S(2)}, u32[]{:S(2)}) collective-permute-start(bf16[512,2048]{0,1:T(8,128)(2,1)S(1)} %collective-permute-done.17), channel_id=1, source_target_pairs={{0,15},{1,0},{2,1},{3,2},{4,3},{5,4},{6,5},{7,6},{8,7},{9,8},{10,9... | collective-permute-start | bytes 6291464 | tf_op jit(solution)/shard_map/ppermute | solution.py:52
  247.0 10.6 %copy-start.4 = (bf16[2560,1024]{0,1:T(8,128)(2,1)S(1)}, bf16[2560,1024]{0,1:T(8,128)(2,1)}, u32[]{:S(2)}) copy-start(bf16[2560,1024]{0,1:T(8,128)(2,1)} %get-tuple-element.8) | copy-start | bytes 15728644
  275.1 8.7 %copy-start.5 = (pred[512,2560]{1,0:T(8,128)(4,1)S(1)}, pred[512,2560]{1,0:T(8,128)(4,1)}, u32[]{:S(2)}) copy-start(pred[512,2560]{1,0:T(8,128)(4,1)} %fusion.41) | copy-start | bytes 3932164
  437.2 30.0 %copy-start.18 = (f32[4]{0:T(128)S(1)}, f32[4]{0:T(128)}, u32[]{:S(2)}) copy-start(f32[4]{0:T(128)} %get-tuple-element.16) | copy-start | bytes 52
  437.2 30.0 %copy-start.19 = (f32[4]{0:T(128)S(1)}, f32[4]{0:T(128)}, u32[]{:S(2)}) copy-start(f32[4]{0:T(128)} %get-tuple-element.17) | copy-start | bytes 52
  498.7 33.9 %copy-start.1 = (bf16[512,1024]{1,0:T(8,128)(2,1)S(1)}, bf16[512,1024]{1,0:T(8,128)(2,1)}, u32[]{:S(2)}) copy-start(bf16[512,1024]{1,0:T(8,128)(2,1)} %param.7) | copy-start | bytes 3145732
Sparse Core Ops, SparseCore 0:
  128.7 52.1 all-gather.1
